TPU v7x, 768 devices: a whole 4x8x12 slice. The times are simulated.
768 devices in a mesh: role: 4 (over y_hi), band: 24 (over y_lo, z), turn: 8 (over x, core).
Axes of the slice: x: 4, y: 8 (y_hi: 4, y_lo: 2; y = y_hi * 2 + y_lo), z: 12, core: 2. Of those that a mesh axis runs over, the one named last changes fastest.
Arguments:
- voltages: bfloat16 [96, 2, 256, 3840], P(('role', 'band'), None, 'turn'), may hold values from -6 to 6
- station_flags: int32 [256], P('turn'), may hold values 0 or 1
- filter_taps: bfloat16 [8, 256, 256], replicated, may hold values from -0.125 to 0.125
- kernel_rows: bfloat16 [96, 1, 32, 256], P(('role', 'band')), may hold values from -0.375 to 0.375
- kernel_cols: bfloat16 [96, 1, 32, 256], P(('role', 'band')), may hold values from -0.375 to 0.375
- cell_index: int32 [2, 12288, 1], P(None, ('role', 'band', 'turn')), may hold values from 0 to 4095
Outputs:
- image: float32 [768, 128], P(('role', 'band', 'turn'))
All inputs are finite; a program needn't handle non-finite values. No bound on the sum of `station_flags` on one device may be relied on, other than what follows from the above.
Results may differ from a plain program's by a relative error of at most 0.0071.
Values may be sent and summed in bfloat16 or wider, within the bound.
A program may use at most 32 MiB of HBM per device.

v0:
```python
import math

import jax
import jax.numpy as jnp
from jax import lax
from jax.sharding import PartitionSpec as P

FINE = 128
NGRID = 4096
MW = 128
ROWS_DEV = 1


def channelize(voltages, station_flags, filter_taps):
    polars, station_rows, sample_width = voltages.shape
    tap_count, two_fine, _ = filter_taps.shape
    block_total = sample_width // two_fine
    frames = block_total - tap_count + 1
    flagged = voltages * station_flags[None, :, None].astype(voltages.dtype)
    blocks = flagged.reshape(polars * station_rows, block_total, two_fine)
    running = jnp.zeros((polars * station_rows * frames, two_fine), jnp.float32)
    for tap_index in range(tap_count):
        segment = blocks[:, tap_index : tap_index + frames, :].reshape(
            polars * station_rows * frames, two_fine
        )
        running = running + jnp.dot(
            segment, filter_taps[tap_index], preferred_element_type=jnp.float32
        )
    fine_count = two_fine // 2
    result = running.astype(jnp.bfloat16).reshape(polars, station_rows, frames, 2, fine_count)
    return jnp.transpose(result, (4, 0, 1, 3, 2)).reshape(
        fine_count, polars, station_rows, 2 * frames
    )


def correlate(spectra):
    frames = spectra.shape[3] // 2
    station_count = spectra.shape[2]
    swapped = jnp.concatenate([-spectra[..., frames:], spectra[..., :frames]], axis=3)
    stacked = jnp.concatenate([spectra, swapped], axis=2)
    products = jnp.einsum("fpsa,fpka->fpsk", spectra, stacked, preferred_element_type=jnp.float32)
    stokes = (products[:, 0] + products[:, 1]) * (1.0 / frames)
    return jnp.stack([stokes[:, :, :station_count], stokes[:, :, station_count:]]).astype(
        jnp.bfloat16
    )


def subgrids(visibility, kernel_rows, kernel_cols):
    fine_local = visibility.shape[1]
    station_count = visibility.shape[2]
    block_count, sub_u, block_width = kernel_rows.shape
    sub_v = kernel_cols.shape[1]
    station_rows = visibility.reshape(2, fine_local, block_count, block_width, station_count)
    partial_value = jnp.einsum(
        "iab,xfibs->xfias", kernel_rows, station_rows, preferred_element_type=jnp.float32
    )
    partial_value = partial_value.reshape(
        2, fine_local, block_count, sub_u, block_count, block_width
    )
    result = jnp.einsum(
        "xfiajc,jdc->xfijad",
        partial_value,
        kernel_cols.astype(jnp.float32),
        precision=lax.Precision.HIGHEST,
    )
    return result.reshape(2, fine_local, block_count * block_count, sub_u * sub_v).astype(
        jnp.bfloat16
    )


def fine_subgrids(spectra, kernel_rows, kernel_cols):

    def one_fine(spec_one):
        return subgrids(correlate(spec_one[None]), kernel_rows, kernel_cols)[:, 0]

    stacked = lax.map(one_fine, spectra)
    return jnp.transpose(stacked, (1, 0, 2, 3))


def phase_table(positions, offset_count, pixels, grid_size):
    offsets = jnp.arange(offset_count, dtype=jnp.int32)
    position = positions[:, None, None] + offsets[None, :, None]
    phase_turns = jnp.mod(position * pixels[None, None, :], grid_size)
    angles = phase_turns.astype(jnp.float32) * (2.0 * math.pi / grid_size)
    return (jnp.cos(angles).astype(jnp.bfloat16), jnp.sin(angles).astype(jnp.bfloat16))


def image_rows(subgrid, positions, row_count, row_total, sub_u, sub_v, col_total, grid_size):
    count_sub = subgrid.shape[1]
    row_pix = jnp.arange(row_count, dtype=jnp.int32) - row_total // 2
    col_pix = jnp.arange(col_total, dtype=jnp.int32) - col_total // 2
    row_cos, row_sin = phase_table(positions[0], sub_u, row_pix, grid_size)
    col_cos, col_sin = phase_table(positions[1], sub_v, col_pix, grid_size)
    sub_cells = subgrid.reshape(2, count_sub, sub_u, sub_v)
    proj_real = (
        jnp.einsum("nal,nab->nbl", row_cos, sub_cells[0], preferred_element_type=jnp.float32)
        - jnp.einsum("nal,nab->nbl", row_sin, sub_cells[1], preferred_element_type=jnp.float32)
    ).astype(jnp.bfloat16)
    proj_imag = (
        jnp.einsum("nal,nab->nbl", row_cos, sub_cells[1], preferred_element_type=jnp.float32)
        + jnp.einsum("nal,nab->nbl", row_sin, sub_cells[0], preferred_element_type=jnp.float32)
    ).astype(jnp.bfloat16)
    return jnp.einsum(
        "nbl,nbm->lm", proj_real, col_cos, preferred_element_type=jnp.float32
    ) - jnp.einsum("nbl,nbm->lm", proj_imag, col_sin, preferred_element_type=jnp.float32)


def local(voltages, station_flags, filter_taps, kernel_rows, kernel_cols, cell_index):
    spectra = channelize(voltages[0], station_flags, filter_taps)
    turned = lax.all_to_all(spectra, "turn", split_axis=0, concat_axis=2, tiled=True)
    subgrid = fine_subgrids(turned, kernel_rows[0], kernel_cols[0])
    sub_u = kernel_rows.shape[2]
    sub_v = kernel_cols.shape[2]
    block_count = kernel_rows.shape[1]
    device_total = lax.axis_size("role") * lax.axis_size("band") * lax.axis_size("turn")
    row_total = ROWS_DEV * device_total
    channel_total = FINE * lax.axis_size("role") * lax.axis_size("band")
    scale_factor = 4.0 / math.sqrt(channel_total * block_count * block_count * sub_u * sub_v)
    flat_grid = subgrid.reshape(2, -1, sub_u * sub_v)
    flat_places = cell_index.reshape(2, -1)
    summed = lax.psum_scatter(
        image_rows(
            flat_grid,
            flat_places,
            row_total // device_total * lax.axis_size(("role", "band", "turn")),
            row_total,
            sub_u,
            sub_v,
            MW,
            NGRID,
        ),
        ("role", "band", "turn"),
        scatter_dimension=0,
        tiled=True,
    )
    return summed * scale_factor


def solution(mesh):
    in_specs = (
        P(("role", "band"), None, "turn", None),
        P("turn"),
        P(),
        P(("role", "band"), None, None, None),
        P(("role", "band"), None, None, None),
        P(None, ("role", "band", "turn"), None),
    )
    out_specs = P(("role", "band", "turn"), None)
    return jax.shard_map(local, mesh=mesh, in_specs=in_specs, out_specs=out_specs, check_vma=False)
```

profile of v0, /device:TPU:1, one launch (start us, length us, event | category | flops | bytes accessed | tf_op | source)
XLA Modules:
  0.0 560.2 jit_solution(13473838578728974914)
XLA Ops:
  6.5 1.5 squeeze.46
  8.0 0.7 convert_element_type.61
  9.0 0.2 fusion.30
  9.2 0.2 convolution_add_fusion.6
  9.4 0.2 convolution_add_fusion.5
  9.7 0.2 convolution_add_fusion.4
  9.9 0.2 convolution_add_fusion.3
  10.2 0.2 convolution_add_fusion.2
  10.4 0.2 convolution_add_fusion.1
  10.7 0.2 fusion.23
  10.9 1.5 copy.14
  12.5 1.7 reshape.208
  14.2 13.8 %all-to-all-start = ((bf16[8,2,8192]{2,1,0:T(2,128)(2,1)}), bf16[8,2,8192]{2,1,0:T(2,128)(2,1)S(1)}, u32[]{:S(2)}, u32[]{:S(2)}) async-start(bf16[8,2,8192]{2,1,0:T(2,128)(2,1)} %reshape.208), calls=%async_computation | async-start | bytes 524288 | tf_op jit(solution)/shard_map/all_to_all | solution.py:110
  28.1 6.4 %all-to-all-done = bf16[8,2,8192]{2,1,0:T(2,128)(2,1)S(1)} async-done(((bf16[8,2,8192]{2,1,0:T(2,128)(2,1)}), bf16[8,2,8192]{2,1,0:T(2,128)(2,1)S(1)}, u32[]{:S(2)}, u32[]{:S(2)}) %all-to-all-start) | async-done | bytes 262176 | tf_op jit(solution)/shard_map/all_to_all | solution.py:110
  34.5 0.5 reshape.209
  35.0 1.2 copy.15
  36.3 0.7 all_to_all.16
  37.0 15.7 %while.10 = (s32[]{:T(128)}, bf16[16,2,1,1024]{3,1,2,0:T(2,128)(2,1)S(1)}, bf16[16,2,256,16]{2,3,1,0:T(8,128)(2,1)S(1)}, bf16[1,32,256]{2,1,0:T(8,128)(2,1)S(1)}...) while((s32[]{:T(128)}, bf16[16,2,1,1024]{3,1,2,0:T(2,128)(2,1)S(1)}, ...), condition=%wide.region_1.2_spmd, body=%wide.region_0.1_spmd.sunk | while | flops 24098820 | bytes 3428465 | solution.py:76
  37.1 0.3 convolution_bitcast_fusion.4
  38.0 0.3 convolution_bitcast_fusion.4
  38.7 0.2 fusion.94
  39.0 0.3 convolution_bitcast_fusion.4
  39.6 0.2 fusion.94
  40.0 0.3 convolution_bitcast_fusion.4
  40.6 0.2 fusion.94
  40.9 0.3 convolution_bitcast_fusion.4
  41.9 0.3 convolution_bitcast_fusion.4
  42.5 0.2 fusion.94
  42.9 0.3 convolution_bitcast_fusion.4
  43.5 0.2 fusion.94
  43.8 0.3 convolution_bitcast_fusion.4
  44.8 0.3 convolution_bitcast_fusion.4
  45.8 0.3 convolution_bitcast_fusion.4
  46.7 0.3 convolution_bitcast_fusion.4
  47.4 0.2 fusion.94
  47.7 0.3 convolution_bitcast_fusion.4
  48.7 0.3 convolution_bitcast_fusion.4
  49.6 0.3 convolution_bitcast_fusion.4
  50.6 0.3 convolution_bitcast_fusion.4
  51.3 0.2 fusion.94
  51.6 0.3 convolution_bitcast_fusion.4
  52.7 0.3 slice_reduce_fusion.1
  53.3 6.0 %fusion.25 = f32[16,32,768]{2,1,0:T(8,128)S(1)} fusion(bf16[16,32,32]{2,1,0:T(8,128)(2,1)S(1)} %squeeze.58, s32[768]{0:T(1024)S(1)} %iota_add_fusion.2, s32[16,32]{1,0:T(8,128)S(1)} %get-tuple-element.52), kind=kOutput, calls=%fused_computation.50 | convolution fusion | flops 31064064 | bytes 1610752 | tf_op jit(solution)/shard_map/nal,nab->nbl/dot_general | solution.py:100
  59.3 6.2 %fusion.26 = f32[16,32,768]{2,1,0:T(8,128)S(1)} fusion(bf16[16,32,32]{2,1,0:T(8,128)(2,1)S(1)} %squeeze.57, s32[768]{0:T(1024)S(1)} %iota_add_fusion.2, s32[16,32]{1,0:T(8,128)S(1)} %get-tuple-element.52), kind=kOutput, calls=%fused_computation.51 | convolution fusion | flops 31064064 | bytes 1610752 | tf_op jit(solution)/shard_map/nal,nab->nbl/dot_general | solution.py:96
  65.5 8.1 %fusion.21 = f32[768,128]{1,0:T(8,128)} fusion(f32[16,32,768]{2,1,0:T(8,128)S(1)} %fusion.25, bf16[16,32,32]{2,1,0:T(8,128)(2,1)S(1)} %squeeze.57, s32[768]{0:T(1024)S(1)} %iota_add_fusion.2, s32[16,32]{1,0:T(8,128)S(1)} %get-tuple-element.52, s32[128]{0:T(128)S(1)} %iota_add_fusion.3, s32[16,32]{1,0:T(8,128)S(1)} %get-tuple-element.51), kind=kOutput, calls=%fused_computation.46 | convolution fusion | flops 133496832 | bytes 2006528 | tf_op jit(solution)/shard_map/nbl,nbm->lm/dot_general | solution.py:105
  73.5 9.3 %fusion.24 = f32[768,128]{1,0:T(8,128)} fusion(f32[768,128]{1,0:T(8,128)} %fusion.21, f32[16,32,768]{2,1,0:T(8,128)S(1)} %fusion.26, bf16[16,32,32]{2,1,0:T(8,128)(2,1)S(1)} %squeeze.58, s32[768]{0:T(1024)S(1)} %iota_add_fusion.2, s32[16,32]{1,0:T(8,128)S(1)} %get-tuple-element.52, s32[128]{0:T(128)S(1)} %iota_add_fusion.3, s32[16,32]{1,0:T(8,128)S(1)} %get-tuple-element.51), kind=kOutput, calls=%fused_computation.49 | convolution fusion | flops 133595136 | bytes 2399744 | tf_op jit(solution)/shard_map/nbl,nbm->lm/dot_general | solution.py:103
  82.9 469.3 %all-reduce.3.cloned.1.call-done = f32[768,128]{1,0:T(8,128)} async-done(((f32[768,128]{1,0:T(8,128)}), f32[768,128]{1,0:T(8,128)}) %all-reduce.3.cloned.1.call-update) | async-done | bytes 393232
  552.2 1.2 dynamic-slice_multiply_fusion
  (142 shorter events, 8.9 us)
Async XLA Ops:
  6.5 2.4 copy-start
  12.4 15.6 %copy-start.2 = (s32[2,16,1]{1,2,0:T(1,128)S(1)}, s32[2,16,1]{1,2,0:T(1,128)}, u32[]{:S(2)}) copy-start(s32[2,16,1]{1,2,0:T(1,128)} %param.13) | copy-start | bytes 388
  14.2 20.3 %all-to-all-start = ((bf16[8,2,8192]{2,1,0:T(2,128)(2,1)}), bf16[8,2,8192]{2,1,0:T(2,128)(2,1)S(1)}, u32[]{:S(2)}, u32[]{:S(2)}) async-start(bf16[8,2,8192]{2,1,0:T(2,128)(2,1)} %reshape.208), calls=%async_computation | async-start | bytes 524288 | tf_op jit(solution)/shard_map/all_to_all | solution.py:110
  28.0 524.2 %all-reduce.3.cloned.1.call-start = ((), (), s32[]{:S(2)}) async-start(), calls=%async_computation.1 | async-start | bytes 786432
  35.0 2.0 copy-start.1
  35.0 2.0 copy-start.3
Sparse Core Ops, SparseCore 0:
  83.0 469.1 all-reduce.2
where the time goes:
time: 561 us; the launch traced here: 560 us
  waiting for transfers between devices  476 us (85%)
  matrix products  41.9 us (7%)
  starting transfers between devices  13.8 us (2%)
  between operations  13.6 us (2%)
  local copies, waits for them, and re-layouts  10.1 us (2%)
    unnamed x2, waiting for transfers between devices  469 us
    all_to_all x1, starting transfers between devices, local(): lax.all_to_all(spectra, 'turn', split_axis=0, concat_axis=2, tiled=True)  13.8 us
  transfers between devices with their start and end apart: 2, of which 2 were waited for; matrix products, arithmetic and copies ran while one was open for 0% of the time, Pallas kernels for 0%

commit v1 on v0

v1 whole, which is shorter than its diff:
```python
import math

import jax
import jax.numpy as jnp
from jax import lax
from jax.experimental import pallas as pl
from jax.experimental.pallas import tpu as pltpu
from jax.sharding import PartitionSpec as P

MESH = pl.DeviceIdType.MESH
F32 = jnp.float32
BF16 = jnp.bfloat16
I32 = jnp.int32

NGRID = 4096
NT, NY, NZ = 8, 8, 12
FINE = 128
FLOC = 16
STLOC = 32
TAPS = 8
FRAMES = 8
SUB = 32
MW = 128
LW = NT * NY * NZ
PIECE = NY * NZ
SCALE = 4.0 / math.sqrt(96 * FINE * SUB * SUB)
CHUNK = 256


def iota(shape, dim):
    return lax.broadcasted_iota(I32, shape, dim)


def trig(turns):
    shifted = turns + 512
    quadrant = shifted >> 10
    x = ((shifted & 1023) - 512).astype(F32) * (2.0 * math.pi / NGRID)
    x2 = x * x
    s = x * (1.0 + x2 * (-1.0 / 6 + x2 * (1.0 / 120 + x2 * (-1.0 / 5040 + x2 * (1.0 / 362880)))))
    c = 1.0 + x2 * (-0.5 + x2 * (1.0 / 24 + x2 * (-1.0 / 720 + x2 * (1.0 / 40320))))
    odd = (quadrant & 1) == 1
    cos = jnp.where(odd, s, c)
    sin = jnp.where(odd, c, s)
    cos = jnp.where(((quadrant + 1) & 2) == 2, -cos, cos)
    sin = jnp.where((quadrant & 2) == 2, -sin, sin)
    return cos, sin


def split(x):
    high = x.astype(BF16)
    return high, (x - high.astype(F32)).astype(BF16)


def channelize(v_ref, flag_ref, taps_ref, xs_ref):
    width = 2 * FINE
    lhs = jnp.concatenate(
        [v_ref[:, t * width : (t + TAPS) * width] for t in range(FRAMES)], axis=0
    )
    out = jnp.dot(lhs, taps_ref[...], preferred_element_type=F32)
    lane = iota((1, 128), 1) & (STLOC - 1)
    flags = jnp.zeros((1, 128), F32)
    for s in range(STLOC):
        flags = jnp.where(lane == s, flag_ref[s].astype(F32), flags)
    turned = (out.T * jnp.concatenate([flags] * 4, axis=1)).astype(BF16)
    for d in range(NT):
        for c in range(2):
            xs_ref[d, c] = turned[c * FINE + d * FLOC : c * FINE + (d + 1) * FLOC, :]


def tables(mt, my, mz, cell_ref, t0_ref, ph_ref, ct_ref):
    lane = iota((1, LW), 1)
    kt = jnp.zeros((1, LW), I32)
    for i in range(1, NT):
        kt = kt + (lane >= PIECE * i).astype(I32)
    j = lane - PIECE * kt
    z = mz + 1 + (j >> 3)
    z = jnp.where(z >= NZ, z - NZ, z)
    y = (my + 1 + (j & 7)) & (NY - 1)
    t = (mt + 1 + kt) & (NT - 1)
    pix = NT * (NZ * y + z) + t - LW // 2
    cos, sin = trig(iota((SUB, LW), 0) * pix)
    cos_hi, cos_lo = split(cos)
    sin_hi, sin_lo = split(sin)
    t0_ref[0:32] = cos_hi
    t0_ref[32:64] = sin_hi
    t0_ref[64:96] = cos_lo
    t0_ref[96:128] = sin_lo
    row = iota((FLOC, LW), 0)
    cell_u = jnp.zeros((FLOC, LW), I32)
    for n in range(FLOC):
        cell_u = jnp.where(row == n, cell_ref[0, n], cell_u)
    cos, sin = trig(cell_u * pix)
    ph_ref[0] = cos
    ph_ref[1] = sin
    lane = iota((1, FLOC * SUB), 1)
    cell_v = jnp.zeros((1, FLOC * SUB), I32)
    for n in range(FLOC):
        cell_v = jnp.where((lane >> 5) == n, cell_ref[1, n], cell_v)
    cell_v = cell_v + (lane & 31)
    cos, sin = trig((iota((MW, FLOC * SUB), 0) - MW // 2) * cell_v)
    ct_ref[:, : FLOC * SUB] = cos.astype(BF16)
    ct_ref[:, FLOC * SUB :] = (-sin).astype(BF16)


def weights(kr_ref, kc_ref, w_ref):
    w_ref[...] = jnp.zeros(w_ref.shape, BF16)
    for side, k_ref in enumerate((kr_ref, kc_ref)):
        k = k_ref[...].astype(F32)
        kt = jnp.concatenate([k] * 4, axis=0).T.astype(BF16)
        for src in range(NT):
            for q in range(4):
                w_ref[
                    src * 128 + q * 32 : src * 128 + (q + 1) * 32,
                    side * 512 + q * 128 : side * 512 + (q + 1) * 128,
                ] = kt[src * 32 : (src + 1) * 32, :]


def subgrids(xr_ref, w_ref, ab_ref, sall_ref):
    lhs = jnp.concatenate(
        [
            jnp.concatenate([xr_ref[src, c, :, g * 128 : (g + 1) * 128] for src in range(NT)], axis=1)
            for g in range(4)
            for c in range(2)
        ],
        axis=0,
    )
    out = jnp.dot(lhs, w_ref[...], preferred_element_type=F32)
    u = out[:, :512]
    v = jnp.concatenate(
        [
            u[(2 * g + 1) * FLOC : (2 * g + 2) * FLOC] if c == 0 else -u[2 * g * FLOC : (2 * g + 1) * FLOC]
            for g in range(4)
            for c in range(2)
        ],
        axis=0,
    )
    odd = ((iota((128, 512), 1) >> 5) & 1) == 1
    real = jnp.where(odd, -v, u)
    imag = jnp.where(odd, u, v)
    for q in range(4):
        part = slice(q * 128, (q + 1) * 128)
        ab_ref[0, q] = real[:, part]
        ab_ref[1, q] = imag[:, part]
        ab_ref[2, q] = out[:, 512 + q * 128 : 512 + (q + 1) * 128]
    same = (iota((128, 128), 0) >> 5) == (iota((128, 128), 1) >> 5)
    for h in range(4):

        def gather(k):
            return jnp.concatenate(
                [
                    ab_ref[k, q, pl.ds(fl, 8, stride=FLOC), :]
                    for fl in range(4 * h, 4 * h + 4)
                    for q in range(4)
                ],
                axis=0,
            )

        b_hi, b_lo = split(jnp.where(same, gather(2), 0.0).T)
        a_hi, a_lo = split(jnp.concatenate([gather(0), gather(1)], axis=1))
        sub = (
            jnp.dot(b_hi, a_hi, preferred_element_type=F32)
            + jnp.dot(b_lo, a_hi, preferred_element_type=F32)
            + jnp.dot(b_hi, a_lo, preferred_element_type=F32)
        ) * (1.0 / FRAMES)
        sub = sub.astype(BF16)
        sall_ref[0, h * 128 : (h + 1) * 128, :] = sub[:, :128]
        sall_ref[1, h * 128 : (h + 1) * 128, :] = sub[:, 128:]


def image_chunk(chunk, sall_ref, t0_ref, ph_ref, ct_ref):
    part = slice(chunk * CHUNK, (chunk + 1) * CHUNK)
    table = t0_ref[:, part]
    g_r = jnp.dot(sall_ref[0], table, preferred_element_type=F32).reshape(FLOC, SUB, CHUNK)
    g_i = jnp.dot(sall_ref[1], table, preferred_element_type=F32).reshape(FLOC, SUB, CHUNK)
    cos = ph_ref[0, :, part][:, None, :]
    sin = ph_ref[1, :, part][:, None, :]
    p_r = (cos * g_r - sin * g_i).astype(BF16).reshape(FLOC * SUB, CHUNK)
    p_i = (cos * g_i + sin * g_r).astype(BF16).reshape(FLOC * SUB, CHUNK)
    image = jnp.dot(ct_ref[...], jnp.concatenate([p_r, p_i], axis=0), preferred_element_type=F32)
    return image.T


def kernel(
    v_ref, flag_ref, taps_ref, kr_ref, kc_ref, cell_ref, out_ref,
    xs_ref, xr_ref, t0_ref, ph_ref, ct_ref, w_ref, ab_ref, sall_ref, img_ref,
    tr_ref, zs_ref, zr_ref, ys_ref, yr_ref,
    own_sem, a_send, a_recv, t_send, t_recv, z_send, z_recv, y_send, y_recv,
):
    role = lax.axis_index("role")
    band = lax.axis_index("band")
    mt = lax.axis_index("turn")
    y_lo = band // NZ
    mz = band % NZ
    my = 2 * role + y_lo

    def turn_of(k):
        return {"turn": (mt + 1 + k) % NT}

    def z_of(k):
        return {"band": y_lo * NZ + (mz + 1 + k) % NZ}

    def y_of(k):
        y = (my + 1 + k) % NY
        return {"role": y // 2, "band": (y % 2) * NZ + mz}

    barrier = pltpu.get_barrier_semaphore()
    for k in range(NT - 1):
        pl.semaphore_signal(barrier, inc=1, device_id=turn_of(k), device_id_type=MESH)
    for k in range(NZ - 1):
        pl.semaphore_signal(barrier, inc=1, device_id=z_of(k), device_id_type=MESH)
    for k in range(NY - 1):
        pl.semaphore_signal(barrier, inc=1, device_id=y_of(k), device_id_type=MESH)

    channelize(v_ref, flag_ref, taps_ref, xs_ref)

    pl.semaphore_wait(barrier, NT + NZ + NY - 3)
    spread = []
    for k in range(NT - 1):
        dest = (mt + 1 + k) % NT
        copy = pltpu.make_async_remote_copy(
            src_ref=xs_ref.at[dest], dst_ref=xr_ref.at[mt],
            send_sem=a_send.at[k], recv_sem=a_recv.at[mt],
            device_id=turn_of(k), device_id_type=MESH,
        )
        copy.start()
        spread.append(copy)
    own = pltpu.make_async_copy(xs_ref.at[mt], xr_ref.at[mt], own_sem)
    own.start()

    tables(mt, my, mz, cell_ref, t0_ref, ph_ref, ct_ref)
    weights(kr_ref, kc_ref, w_ref)

    own.wait()
    for k in range(NT - 1):
        src = (mt + 1 + k) % NT
        pltpu.make_async_remote_copy(
            src_ref=xs_ref.at[src], dst_ref=xr_ref.at[src],
            send_sem=a_send.at[k], recv_sem=a_recv.at[src],
            device_id=turn_of(k), device_id_type=MESH,
        ).wait_recv()

    subgrids(xr_ref, w_ref, ab_ref, sall_ref)

    def turn_copy(k):
        return pltpu.make_async_remote_copy(
            src_ref=img_ref.at[pl.ds(k * PIECE, PIECE), :], dst_ref=tr_ref.at[k],
            send_sem=t_send.at[k], recv_sem=t_recv.at[k],
            device_id=turn_of(k), device_id_type=MESH,
        )

    turn_copies = []
    done = 0
    for chunk in range(LW // CHUNK):
        rows = image_chunk(chunk, sall_ref, t0_ref, ph_ref, ct_ref)
        img_ref[chunk * CHUNK : (chunk + 1) * CHUNK, :] = rows.astype(BF16)
        while done < NT - 1 and (done + 1) * PIECE <= (chunk + 1) * CHUNK:
            copy = turn_copy(done)
            copy.start()
            turn_copies.append(copy)
            done += 1
    total = rows[CHUNK - PIECE :, :]
    for k in range(NT - 1):
        turn_copies[k].wait_recv()
        total = total + tr_ref[k].astype(F32)

    zs_ref[...] = total.reshape(NZ, NY, MW)
    z_copies = []
    for k in range(NZ - 1):
        copy = pltpu.make_async_remote_copy(
            src_ref=zs_ref.at[k], dst_ref=zr_ref.at[k],
            send_sem=z_send.at[k], recv_sem=z_recv.at[k],
            device_id=z_of(k), device_id_type=MESH,
        )
        copy.start()
        z_copies.append(copy)
    total = total[(NZ - 1) * NY :, :]
    for k in range(NZ - 1):
        z_copies[k].wait_recv()
        total = total + zr_ref[k]

    y_copies = []
    for k in range(NY):
        ys_ref[k] = total[k : k + 1, :]
    for k in range(NY - 1):
        copy = pltpu.make_async_remote_copy(
            src_ref=ys_ref.at[k], dst_ref=yr_ref.at[k],
            send_sem=y_send.at[k], recv_sem=y_recv.at[k],
            device_id=y_of(k), device_id_type=MESH,
        )
        copy.start()
        y_copies.append(copy)
    final = total[NY - 1 : NY, :]
    for k in range(NY - 1):
        y_copies[k].wait_recv()
        final = final + yr_ref[k]
    out_ref[...] = final * SCALE
    for copy in spread + turn_copies + z_copies + y_copies:
        copy.wait_send()


def local(voltages, station_flags, filter_taps, kernel_rows, kernel_cols, cell_index):
    vmem = pl.BlockSpec(memory_space=pltpu.VMEM)
    smem = pl.BlockSpec(memory_space=pltpu.SMEM)
    dma = pltpu.SemaphoreType.DMA
    return pl.pallas_call(
        kernel,
        out_shape=jax.ShapeDtypeStruct((1, MW), F32),
        in_specs=[vmem, smem, vmem, vmem, vmem, smem],
        out_specs=vmem,
        scratch_shapes=[
            pltpu.VMEM((NT, 2, FLOC, 512), BF16),
            pltpu.VMEM((NT, 2, FLOC, 512), BF16),
            pltpu.VMEM((128, LW), BF16),
            pltpu.VMEM((2, FLOC, LW), F32),
            pltpu.VMEM((MW, 2 * FLOC * SUB), BF16),
            pltpu.VMEM((1024, 1024), BF16),
            pltpu.VMEM((3, 4, 128, 128), F32),
            pltpu.VMEM((2, FLOC * SUB, 128), BF16),
            pltpu.VMEM((LW, MW), BF16),
            pltpu.VMEM((NT - 1, PIECE, MW), BF16),
            pltpu.VMEM((NZ, NY, MW), F32),
            pltpu.VMEM((NZ - 1, NY, MW), F32),
            pltpu.VMEM((NY, 1, MW), F32),
            pltpu.VMEM((NY - 1, 1, MW), F32),
            dma,
            dma((NT - 1,)),
            dma((NT,)),
            dma((NT - 1,)),
            dma((NT - 1,)),
            dma((NZ - 1,)),
            dma((NZ - 1,)),
            dma((NY - 1,)),
            dma((NY - 1,)),
        ],
        compiler_params=pltpu.CompilerParams(collective_id=0, has_side_effects=True),
    )(
        voltages.reshape(2 * STLOC, -1),
        station_flags,
        filter_taps.reshape(TAPS * 2 * FINE, 2 * FINE),
        kernel_rows.reshape(SUB, -1),
        kernel_cols.reshape(SUB, -1),
        cell_index.reshape(2, FLOC),
    )


def solution(mesh):
    in_specs = (
        P(("role", "band"), None, "turn", None),
        P("turn"),
        P(),
        P(("role", "band"), None, None, None),
        P(("role", "band"), None, None, None),
        P(None, ("role", "band", "turn"), None),
    )
    out_specs = P(("role", "band", "turn"), None)
    return jax.shard_map(local, mesh=mesh, in_specs=in_specs, out_specs=out_specs, check_vma=False)
```

time: 561 us -> 44.2 us (0.08)
  waiting for transfers between devices: 476 us -> 0 us
  Pallas kernels: 0 us -> 42.9 us
  matrix products: 41.9 us -> 0 us
  starting transfers between devices: 13.8 us -> 0 us
  between operations: 13.6 us -> 0.01 us
  local copies, waits for them, and re-layouts: 10.1 us -> 1.19 us
    unnamed x2 -> x0, waiting for transfers between devices: 469 us -> none
    pallas_call x0 -> x1, Pallas kernels: none -> 42.9 us  [local(): pl.pallas_call(kernel, out_shape=jax.ShapeDtypeStruct((1, MW), F32), in_s...]
    dot_general x60 -> x0, matrix products: 41.9 us -> none  [the longest x1 9.31 us: image_rows(): jnp.einsum('nbl,nbm->lm', proj_real, col_cos, preferred_element_type=jnp....]
    all_to_all x1 -> x0, starting transfers between devices: 13.8 us -> none  [local(): lax.all_to_all(spectra, 'turn', split_axis=0, concat_axis=2, tiled=True)]
    all_to_all x1 -> x0, waiting for transfers between devices: 6.37 us -> none  [local(): lax.all_to_all(spectra, 'turn', split_axis=0, concat_axis=2, tiled=True)]
  transfers between devices with their start and end apart: 2 -> 0, of which waited for: 2 -> 0; matrix products, arithmetic and copies ran while one was open for 0% -> 0% of each run, Pallas kernels for 0% -> 0%
where the time goes in v1:
time: 44.2 us; the launch traced here: 44.1 us
  Pallas kernels  42.9 us (97%)
  local copies, waits for them, and re-layouts  1.19 us (3%)
    pallas_call x1, Pallas kernels, local(): pl.pallas_call(kernel, out_shape=jax.ShapeDtypeStruct((1, MW), F32), in_s...  42.9 us
    unnamed x1, local copies, waits for them, and re-layouts  1.19 us

profile of v1, /device:TPU:1, one launch (start us, length us, event | category | flops | bytes accessed | tf_op | source)
XLA Modules:
  0.0 44.1 jit_solution(5270564191027328291)
XLA Ops:
  0.0 42.9 %shard_map.64 = f32[1,128]{1,0:T(1,128)} custom-call(bf16[64,3840]{1,0:T(8,128)(2,1)} %bitcast.6, s32[32]{0:T(128)} %flag_ref.1, bf16[2048,256]{1,0:T(8,128)(2,1)} %bitcast.5, bf16[32,256]{1,0:T(8,128)(2,1)} %bitcast.7, bf16[32,256]{1,0:T(8,128)(2,1)} %bitcast.8, s32[2,16]{1,0:T(2,128)} %bitcast.9), custom_call_target="tpu_custom_call" | custom-call | tf_op jit(solution)/shard_map/pallas_call | solution.py:305
  42.9 1.2 %copy.8 = f32[1,128]{1,0:T(1,128)} copy(f32[1,128]{1,0:T(1,128)} %shard_map.64) | data formatting | bytes 1024

commit v2 on v1

--- a/solution.py
+++ b/solution.py
@@ -181,10 +181,11 @@
 
 
 def kernel(
-    v_ref, flag_ref, taps_ref, kr_ref, kc_ref, cell_ref, out_ref,
+    v_hbm, flag_hbm, taps_hbm, kr_hbm, kc_hbm, cell_hbm, out_ref,
+    v_ref, flag_ref, taps_ref, kr_ref, kc_ref, cell_ref,
     xs_ref, xr_ref, t0_ref, ph_ref, ct_ref, w_ref, ab_ref, sall_ref, img_ref,
     tr_ref, zs_ref, zr_ref, ys_ref, yr_ref,
-    own_sem, a_send, a_recv, t_send, t_recv, z_send, z_recv, y_send, y_recv,
+    in_sem, near, mid, far, own_sem, a_send, a_recv, t_send, t_recv, z_send, z_recv, y_send, y_recv,
 ):
     role = lax.axis_index("role")
     band = lax.axis_index("band")
@@ -203,17 +204,33 @@
         y = (my + 1 + k) % NY
         return {"role": y // 2, "band": (y % 2) * NZ + mz}
 
+    def tell(sem, device):
+        pl.semaphore_signal(sem, inc=1, device_id=device, device_id_type=MESH)
+
+    fetches = [
+        pltpu.make_async_copy(src, dst, in_sem.at[i])
+        for i, (src, dst) in enumerate(
+            (
+                (v_hbm, v_ref), (taps_hbm, taps_ref), (flag_hbm, flag_ref),
+                (kr_hbm, kr_ref), (kc_hbm, kc_ref), (cell_hbm, cell_ref),
+            )
+        )
+    ]
+    for fetch in fetches:
+        fetch.start()
+
     barrier = pltpu.get_barrier_semaphore()
     for k in range(NT - 1):
-        pl.semaphore_signal(barrier, inc=1, device_id=turn_of(k), device_id_type=MESH)
-    for k in range(NZ - 1):
-        pl.semaphore_signal(barrier, inc=1, device_id=z_of(k), device_id_type=MESH)
-    for k in range(NY - 1):
-        pl.semaphore_signal(barrier, inc=1, device_id=y_of(k), device_id_type=MESH)
-
+        tell(barrier, turn_of(k))
+    for step in (1, -1):
+        tell(barrier, z_of(step - 1))
+        tell(barrier, y_of(step - 1))
+
+    for fetch in fetches[:3]:
+        fetch.wait()
     channelize(v_ref, flag_ref, taps_ref, xs_ref)
 
-    pl.semaphore_wait(barrier, NT + NZ + NY - 3)
+    pl.semaphore_wait(barrier, NT + 3)
     spread = []
     for k in range(NT - 1):
         dest = (mt + 1 + k) % NT
@@ -226,9 +243,19 @@
         spread.append(copy)
     own = pltpu.make_async_copy(xs_ref.at[mt], xr_ref.at[mt], own_sem)
     own.start()
-
+    for step in (1, -1):
+        tell(near, z_of(step - 1))
+        tell(near, y_of(step - 1))
+
+    for fetch in fetches[3:]:
+        fetch.wait()
     tables(mt, my, mz, cell_ref, t0_ref, ph_ref, ct_ref)
     weights(kr_ref, kc_ref, w_ref)
+
+    pl.semaphore_wait(near, 4)
+    for step in (2, -2):
+        tell(mid, z_of(step - 1))
+        tell(mid, y_of(step - 1))
 
     own.wait()
     for k in range(NT - 1):
@@ -238,6 +265,10 @@
             send_sem=a_send.at[k], recv_sem=a_recv.at[src],
             device_id=turn_of(k), device_id_type=MESH,
         ).wait_recv()
+
+    pl.semaphore_wait(mid, 4)
+    for step in (2, -2):
+        tell(far, z_of(step - 1))
 
     subgrids(xr_ref, w_ref, ab_ref, sall_ref)
 
@@ -258,12 +289,13 @@
             copy.start()
             turn_copies.append(copy)
             done += 1
+    pl.semaphore_wait(far, 2)
     total = rows[CHUNK - PIECE :, :]
     for k in range(NT - 1):
         turn_copies[k].wait_recv()
         total = total + tr_ref[k].astype(F32)
 
-    zs_ref[...] = total.reshape(NZ, NY, MW)
+    zs_ref[...] = total.astype(BF16).reshape(NZ, NY, MW)
     z_copies = []
     for k in range(NZ - 1):
         copy = pltpu.make_async_remote_copy(
@@ -276,7 +308,7 @@
     total = total[(NZ - 1) * NY :, :]
     for k in range(NZ - 1):
         z_copies[k].wait_recv()
-        total = total + zr_ref[k]
+        total = total + zr_ref[k].astype(F32)
 
     y_copies = []
     for k in range(NY):
@@ -300,14 +332,20 @@
 
 def local(voltages, station_flags, filter_taps, kernel_rows, kernel_cols, cell_index):
     vmem = pl.BlockSpec(memory_space=pltpu.VMEM)
-    smem = pl.BlockSpec(memory_space=pltpu.SMEM)
+    hbm = pl.BlockSpec(memory_space=pl.ANY)
     dma = pltpu.SemaphoreType.DMA
     return pl.pallas_call(
         kernel,
         out_shape=jax.ShapeDtypeStruct((1, MW), F32),
-        in_specs=[vmem, smem, vmem, vmem, vmem, smem],
+        in_specs=[hbm] * 6,
         out_specs=vmem,
         scratch_shapes=[
+            pltpu.VMEM((2 * STLOC, (FRAMES + TAPS - 1) * 2 * FINE), BF16),
+            pltpu.SMEM((STLOC,), I32),
+            pltpu.VMEM((TAPS * 2 * FINE, 2 * FINE), BF16),
+            pltpu.VMEM((SUB, 256), BF16),
+            pltpu.VMEM((SUB, 256), BF16),
+            pltpu.SMEM((2, FLOC), I32),
             pltpu.VMEM((NT, 2, FLOC, 512), BF16),
             pltpu.VMEM((NT, 2, FLOC, 512), BF16),
             pltpu.VMEM((128, LW), BF16),
@@ -318,10 +356,14 @@
             pltpu.VMEM((2, FLOC * SUB, 128), BF16),
             pltpu.VMEM((LW, MW), BF16),
             pltpu.VMEM((NT - 1, PIECE, MW), BF16),
-            pltpu.VMEM((NZ, NY, MW), F32),
-            pltpu.VMEM((NZ - 1, NY, MW), F32),
+            pltpu.VMEM((NZ, NY, MW), BF16),
+            pltpu.VMEM((NZ - 1, NY, MW), BF16),
             pltpu.VMEM((NY, 1, MW), F32),
             pltpu.VMEM((NY - 1, 1, MW), F32),
+            dma((6,)),
+            pltpu.SemaphoreType.REGULAR,
+            pltpu.SemaphoreType.REGULAR,
+            pltpu.SemaphoreType.REGULAR,
             dma,
             dma((NT - 1,)),
             dma((NT,)),

time: 44.2 us -> 40.9 us (0.925)
  Pallas kernels: 42.9 us -> 39.5 us
    pallas_call x1, Pallas kernels: 42.9 us -> 39.5 us  [local(): pl.pallas_call(kernel, out_shape=jax.ShapeDtypeStruct((1, MW), F32), in_s...]
where the time goes in v2:
time: 40.9 us; the launch traced here: 40.7 us
  Pallas kernels  39.5 us (97%)
  local copies, waits for them, and re-layouts  1.19 us (3%)
    pallas_call x1, Pallas kernels, local(): pl.pallas_call(kernel, out_shape=jax.ShapeDtypeStruct((1, MW), F32), in_s...  39.5 us
    unnamed x1, local copies, waits for them, and re-layouts  1.19 us

profile of v2, /device:TPU:1, one launch (start us, length us, event | category | flops | bytes accessed | tf_op | source)
XLA Modules:
  0.0 40.7 jit_solution(13467134178055262951)
XLA Ops:
  0.0 39.5 %shard_map.64 = f32[1,128]{1,0:T(1,128)} custom-call(bf16[64,3840]{1,0:T(8,128)(2,1)} %bitcast.6, s32[32]{0:T(128)} %flag_hbm.1, bf16[2048,256]{1,0:T(8,128)(2,1)} %bitcast.5, bf16[32,256]{1,0:T(8,128)(2,1)} %bitcast.7, bf16[32,256]{1,0:T(8,128)(2,1)} %bitcast.8, s32[2,16]{1,0:T(2,128)} %bitcast.9), custom_call_target="tpu_custom_call" | custom-call | tf_op jit(solution)/shard_map/pallas_call | solution.py:337
  39.5 1.2 %copy.8 = f32[1,128]{1,0:T(1,128)} copy(f32[1,128]{1,0:T(1,128)} %shard_map.64) | data formatting | bytes 1024

commit v3 on v2

--- a/solution.py
+++ b/solution.py
@@ -25,6 +25,14 @@
 PIECE = NY * NZ
 SCALE = 4.0 / math.sqrt(96 * FINE * SUB * SUB)
 CHUNK = 256
+TURNS = ((2, 0), (2, 1), (1, 0), (1, 1), (3, 0), (3, 1), (0, 1), (0, 0))
+ROWS_Z = (6, 5, 7, 4, 8, 3, 9, 2, 10, 1, 11, 0)
+ROWS_Y = (4, 3, 5, 2, 6, 1, 7, 0)
+
+
+def turn_at(mt, k):
+    step, flip = TURNS[k]
+    return (((mt >> 1) + step) & 3) * 2 + ((mt & 1) ^ flip)
 
 
 def iota(shape, dim):
@@ -61,7 +69,7 @@
     flags = jnp.zeros((1, 128), F32)
     for s in range(STLOC):
         flags = jnp.where(lane == s, flag_ref[s].astype(F32), flags)
-    turned = (out.T * jnp.concatenate([flags] * 4, axis=1)).astype(BF16)
+    turned = out.astype(BF16).T * jnp.concatenate([flags] * 4, axis=1).astype(BF16)
     for d in range(NT):
         for c in range(2):
             xs_ref[d, c] = turned[c * FINE + d * FLOC : c * FINE + (d + 1) * FLOC, :]
@@ -73,10 +81,16 @@
     for i in range(1, NT):
         kt = kt + (lane >= PIECE * i).astype(I32)
     j = lane - PIECE * kt
-    z = mz + 1 + (j >> 3)
-    z = jnp.where(z >= NZ, z - NZ, z)
-    y = (my + 1 + (j & 7)) & (NY - 1)
-    t = (mt + 1 + kt) & (NT - 1)
+    kz, ky = j >> 3, j & 7
+    z = jnp.zeros((1, LW), I32) + mz
+    for i, step in enumerate(ROWS_Z):
+        z = jnp.where(kz == i, lax.rem(mz + step, NZ), z)
+    y = jnp.zeros((1, LW), I32) + my
+    for i, step in enumerate(ROWS_Y):
+        y = jnp.where(ky == i, (my + step) & (NY - 1), y)
+    t = jnp.zeros((1, LW), I32) + mt
+    for i in range(NT):
+        t = jnp.where(kt == i, turn_at(mt, i), t)
     pix = NT * (NZ * y + z) + t - LW // 2
     cos, sin = trig(iota((SUB, LW), 0) * pix)
     cos_hi, cos_lo = split(cos)
@@ -115,16 +129,22 @@
                 ] = kt[src * 32 : (src + 1) * 32, :]
 
 
-def subgrids(xr_ref, w_ref, ab_ref, sall_ref):
+def stations(chip, xr_ref, w_ref):
     lhs = jnp.concatenate(
         [
-            jnp.concatenate([xr_ref[src, c, :, g * 128 : (g + 1) * 128] for src in range(NT)], axis=1)
+            jnp.concatenate(
+                [xr_ref[2 * chip + core, c, :, g * 128 : (g + 1) * 128] for core in range(2)], axis=1
+            )
             for g in range(4)
             for c in range(2)
         ],
         axis=0,
     )
-    out = jnp.dot(lhs, w_ref[...], preferred_element_type=F32)
+    rows = pl.ds(pl.multiple_of(chip * 256, 256), 256)
+    return jnp.dot(lhs, w_ref[rows, :], preferred_element_type=F32)
+
+
+def subgrids(out, ab_ref, sall_ref):
     u = out[:, :512]
     v = jnp.concatenate(
         [
@@ -190,19 +210,19 @@
     role = lax.axis_index("role")
     band = lax.axis_index("band")
     mt = lax.axis_index("turn")
-    y_lo = band // NZ
-    mz = band % NZ
+    y_lo = (band >= NZ).astype(I32)
+    mz = band - NZ * y_lo
     my = 2 * role + y_lo
 
     def turn_of(k):
-        return {"turn": (mt + 1 + k) % NT}
-
-    def z_of(k):
-        return {"band": y_lo * NZ + (mz + 1 + k) % NZ}
-
-    def y_of(k):
-        y = (my + 1 + k) % NY
-        return {"role": y // 2, "band": (y % 2) * NZ + mz}
+        return {"turn": turn_at(mt, k)}
+
+    def z_of(step):
+        return {"band": y_lo * NZ + lax.rem(mz + step, NZ)}
+
+    def y_of(step):
+        y = (my + step) & (NY - 1)
+        return {"role": y >> 1, "band": (y & 1) * NZ + mz}
 
     def tell(sem, device):
         pl.semaphore_signal(sem, inc=1, device_id=device, device_id_type=MESH)
@@ -223,8 +243,8 @@
     for k in range(NT - 1):
         tell(barrier, turn_of(k))
     for step in (1, -1):
-        tell(barrier, z_of(step - 1))
-        tell(barrier, y_of(step - 1))
+        tell(barrier, z_of(step + NZ))
+        tell(barrier, y_of(step))
 
     for fetch in fetches[:3]:
         fetch.wait()
@@ -233,7 +253,7 @@
     pl.semaphore_wait(barrier, NT + 3)
     spread = []
     for k in range(NT - 1):
-        dest = (mt + 1 + k) % NT
+        dest = turn_at(mt, k)
         copy = pltpu.make_async_remote_copy(
             src_ref=xs_ref.at[dest], dst_ref=xr_ref.at[mt],
             send_sem=a_send.at[k], recv_sem=a_recv.at[mt],
@@ -244,8 +264,8 @@
     own = pltpu.make_async_copy(xs_ref.at[mt], xr_ref.at[mt], own_sem)
     own.start()
     for step in (1, -1):
-        tell(near, z_of(step - 1))
-        tell(near, y_of(step - 1))
+        tell(near, z_of(step + NZ))
+        tell(near, y_of(step))
 
     for fetch in fetches[3:]:
         fetch.wait()
@@ -254,23 +274,31 @@
 
     pl.semaphore_wait(near, 4)
     for step in (2, -2):
-        tell(mid, z_of(step - 1))
-        tell(mid, y_of(step - 1))
+        tell(mid, z_of(step + NZ))
+        tell(mid, y_of(step))
 
     own.wait()
-    for k in range(NT - 1):
-        src = (mt + 1 + k) % NT
+
+    def arrived(k):
+        src = turn_at(mt, k)
         pltpu.make_async_remote_copy(
             src_ref=xs_ref.at[src], dst_ref=xr_ref.at[src],
             send_sem=a_send.at[k], recv_sem=a_recv.at[src],
             device_id=turn_of(k), device_id_type=MESH,
         ).wait_recv()
 
+    out = None
+    for group in ((6,), (2, 3), (4, 5), (0, 1)):
+        for k in group:
+            arrived(k)
+        term = stations(turn_at(mt, group[0]) >> 1, xr_ref, w_ref)
+        out = term if out is None else out + term
+
     pl.semaphore_wait(mid, 4)
     for step in (2, -2):
-        tell(far, z_of(step - 1))
-
-    subgrids(xr_ref, w_ref, ab_ref, sall_ref)
+        tell(far, z_of(step + NZ))
+
+    subgrids(out, ab_ref, sall_ref)
 
     def turn_copy(k):
         return pltpu.make_async_remote_copy(
@@ -301,7 +329,7 @@
         copy = pltpu.make_async_remote_copy(
             src_ref=zs_ref.at[k], dst_ref=zr_ref.at[k],
             send_sem=z_send.at[k], recv_sem=z_recv.at[k],
-            device_id=z_of(k), device_id_type=MESH,
+            device_id=z_of(ROWS_Z[k]), device_id_type=MESH,
         )
         copy.start()
         z_copies.append(copy)
@@ -317,7 +345,7 @@
         copy = pltpu.make_async_remote_copy(
             src_ref=ys_ref.at[k], dst_ref=yr_ref.at[k],
             send_sem=y_send.at[k], recv_sem=y_recv.at[k],
-            device_id=y_of(k), device_id_type=MESH,
+            device_id=y_of(ROWS_Y[k]), device_id_type=MESH,
         )
         copy.start()
         y_copies.append(copy)
@@ -374,14 +402,14 @@
             dma((NY - 1,)),
             dma((NY - 1,)),
         ],
-        compiler_params=pltpu.CompilerParams(collective_id=0, has_side_effects=True),
+        compiler_params=pltpu.CompilerParams(collective_id=0, has_side_effects=True, vmem_limit_bytes=24 << 20),
     )(
-        voltages.reshape(2 * STLOC, -1),
-        station_flags,
-        filter_taps.reshape(TAPS * 2 * FINE, 2 * FINE),
-        kernel_rows.reshape(SUB, -1),
-        kernel_cols.reshape(SUB, -1),
-        cell_index.reshape(2, FLOC),
+        pltpu.with_memory_space_constraint(voltages.reshape(2 * STLOC, -1), pltpu.HBM),
+        pltpu.with_memory_space_constraint(station_flags, pltpu.HBM),
+        pltpu.with_memory_space_constraint(filter_taps.reshape(TAPS * 2 * FINE, 2 * FINE), pltpu.HBM),
+        pltpu.with_memory_space_constraint(kernel_rows.reshape(SUB, -1), pltpu.HBM),
+        pltpu.with_memory_space_constraint(kernel_cols.reshape(SUB, -1), pltpu.HBM),
+        pltpu.with_memory_space_constraint(cell_index.reshape(2, FLOC), pltpu.HBM),
     )
 
 

time: 40.9 us -> 39.5 us (0.966)
  local copies, waits for them, and re-layouts: 1.19 us -> 0.51 us
  Pallas kernels: 39.5 us -> 38.9 us
    unnamed x1, local copies, waits for them, and re-layouts: 1.19 us -> 0.51 us
    pallas_call x1, Pallas kernels: 39.5 us -> 38.9 us  [local(): pl.pallas_call(kernel, out_shape=jax.ShapeDtypeStruct((1, MW), F32), in_s...]
where the time goes in v3:
time: 39.5 us; the launch traced here: 39.4 us
  Pallas kernels  38.9 us (98%)
  local copies, waits for them, and re-layouts  0.51 us (1%)
    pallas_call x1, Pallas kernels, local(): pl.pallas_call(kernel, out_shape=jax.ShapeDtypeStruct((1, MW), F32), in_s...  38.9 us

profile of v3, /device:TPU:1, one launch (start us, length us, event | category | flops | bytes accessed | tf_op | source)
XLA Modules:
  0.0 39.4 jit_solution(13182840552042171088)
XLA Ops:
  0.0 38.9 %shard_map.64 = f32[1,128]{1,0:T(1,128)S(1)} custom-call(bf16[64,3840]{1,0:T(8,128)(2,1)} %bitcast.6, s32[32]{0:T(128)} %flag_hbm.1, bf16[2048,256]{1,0:T(8,128)(2,1)} %bitcast.5, bf16[32,256]{1,0:T(8,128)(2,1)} %bitcast.7, bf16[32,256]{1,0:T(8,128)(2,1)} %bitcast.8, s32[2,16]{1,0:T(2,128)} %bitcast.9), custom_call_target="tpu_custom_call" | custom-call | tf_op jit(solution)/shard_map/pallas_call | solution.py:365
  38.9 0.5 %copy.8 = f32[1,128]{1,0:T(1,128)} copy(f32[1,128]{1,0:T(1,128)S(1)} %shard_map.64) | data formatting | bytes 1024

commit v4 on v3

--- a/solution.py
+++ b/solution.py
@@ -24,7 +24,7 @@
 LW = NT * NY * NZ
 PIECE = NY * NZ
 SCALE = 4.0 / math.sqrt(96 * FINE * SUB * SUB)
-CHUNK = 256
+EDGES = (0, 128, 384, 768)
 TURNS = ((2, 0), (2, 1), (1, 0), (1, 1), (3, 0), (3, 1), (0, 1), (0, 0))
 ROWS_Z = (6, 5, 7, 4, 8, 3, 9, 2, 10, 1, 11, 0)
 ROWS_Y = (4, 3, 5, 2, 6, 1, 7, 0)
@@ -187,15 +187,16 @@
         sall_ref[1, h * 128 : (h + 1) * 128, :] = sub[:, 128:]
 
 
-def image_chunk(chunk, sall_ref, t0_ref, ph_ref, ct_ref):
-    part = slice(chunk * CHUNK, (chunk + 1) * CHUNK)
+def image_chunk(start, stop, sall_ref, t0_ref, ph_ref, ct_ref):
+    width = stop - start
+    part = slice(start, stop)
     table = t0_ref[:, part]
-    g_r = jnp.dot(sall_ref[0], table, preferred_element_type=F32).reshape(FLOC, SUB, CHUNK)
-    g_i = jnp.dot(sall_ref[1], table, preferred_element_type=F32).reshape(FLOC, SUB, CHUNK)
+    g_r = jnp.dot(sall_ref[0], table, preferred_element_type=F32).reshape(FLOC, SUB, width)
+    g_i = jnp.dot(sall_ref[1], table, preferred_element_type=F32).reshape(FLOC, SUB, width)
     cos = ph_ref[0, :, part][:, None, :]
     sin = ph_ref[1, :, part][:, None, :]
-    p_r = (cos * g_r - sin * g_i).astype(BF16).reshape(FLOC * SUB, CHUNK)
-    p_i = (cos * g_i + sin * g_r).astype(BF16).reshape(FLOC * SUB, CHUNK)
+    p_r = (cos * g_r - sin * g_i).astype(BF16).reshape(FLOC * SUB, width)
+    p_i = (cos * g_i + sin * g_r).astype(BF16).reshape(FLOC * SUB, width)
     image = jnp.dot(ct_ref[...], jnp.concatenate([p_r, p_i], axis=0), preferred_element_type=F32)
     return image.T
 
@@ -309,16 +310,16 @@
 
     turn_copies = []
     done = 0
-    for chunk in range(LW // CHUNK):
-        rows = image_chunk(chunk, sall_ref, t0_ref, ph_ref, ct_ref)
-        img_ref[chunk * CHUNK : (chunk + 1) * CHUNK, :] = rows.astype(BF16)
-        while done < NT - 1 and (done + 1) * PIECE <= (chunk + 1) * CHUNK:
+    for start, stop in zip(EDGES, EDGES[1:]):
+        rows = image_chunk(start, stop, sall_ref, t0_ref, ph_ref, ct_ref)
+        img_ref[start:stop, :] = rows.astype(BF16)
+        while done < NT - 1 and (done + 1) * PIECE <= stop:
             copy = turn_copy(done)
             copy.start()
             turn_copies.append(copy)
             done += 1
     pl.semaphore_wait(far, 2)
-    total = rows[CHUNK - PIECE :, :]
+    total = rows[rows.shape[0] - PIECE :, :]
     for k in range(NT - 1):
         turn_copies[k].wait_recv()
         total = total + tr_ref[k].astype(F32)

time: 39.5 us -> 39.3 us (level)
  no operation moved by 1% of the time
where the time goes in v4:
time: 39.3 us; the launch traced here: 39.2 us
  Pallas kernels  38.7 us (98%)
  local copies, waits for them, and re-layouts  0.51 us (1%)
    pallas_call x1, Pallas kernels, local(): pl.pallas_call(kernel, out_shape=jax.ShapeDtypeStruct((1, MW), F32), in_s...  38.7 us

profile of v4, /device:TPU:1, one launch (start us, length us, event | category | flops | bytes accessed | tf_op | source)
XLA Modules:
  0.0 39.2 jit_solution(3390157240263541820)
XLA Ops:
  0.0 38.7 %shard_map.64 = f32[1,128]{1,0:T(1,128)S(1)} custom-call(bf16[64,3840]{1,0:T(8,128)(2,1)} %bitcast.6, s32[32]{0:T(128)} %flag_hbm.1, bf16[2048,256]{1,0:T(8,128)(2,1)} %bitcast.5, bf16[32,256]{1,0:T(8,128)(2,1)} %bitcast.7, bf16[32,256]{1,0:T(8,128)(2,1)} %bitcast.8, s32[2,16]{1,0:T(2,128)} %bitcast.9), custom_call_target="tpu_custom_call" | custom-call | tf_op jit(solution)/shard_map/pallas_call | solution.py:366
  38.7 0.5 %copy.8 = f32[1,128]{1,0:T(1,128)} copy(f32[1,128]{1,0:T(1,128)S(1)} %shard_map.64) | data formatting | bytes 1024

commit v5 on v4

--- a/solution.py
+++ b/solution.py
@@ -340,20 +340,19 @@
         total = total + zr_ref[k].astype(F32)
 
     y_copies = []
-    for k in range(NY):
-        ys_ref[k] = total[k : k + 1, :]
+    ys_ref[...] = total
+    yr_ref[NY - 1 :, :] = total[NY - 1 :, :]
     for k in range(NY - 1):
         copy = pltpu.make_async_remote_copy(
-            src_ref=ys_ref.at[k], dst_ref=yr_ref.at[k],
+            src_ref=ys_ref.at[pl.ds(k, 1), :], dst_ref=yr_ref.at[pl.ds(k, 1), :],
             send_sem=y_send.at[k], recv_sem=y_recv.at[k],
             device_id=y_of(ROWS_Y[k]), device_id_type=MESH,
         )
         copy.start()
         y_copies.append(copy)
-    final = total[NY - 1 : NY, :]
-    for k in range(NY - 1):
-        y_copies[k].wait_recv()
-        final = final + yr_ref[k]
+    for copy in y_copies:
+        copy.wait_recv()
+    final = jnp.sum(yr_ref[...], axis=0, keepdims=True)
     out_ref[...] = final * SCALE
     for copy in spread + turn_copies + z_copies + y_copies:
         copy.wait_send()
@@ -387,8 +386,8 @@
             pltpu.VMEM((NT - 1, PIECE, MW), BF16),
             pltpu.VMEM((NZ, NY, MW), BF16),
             pltpu.VMEM((NZ - 1, NY, MW), BF16),
-            pltpu.VMEM((NY, 1, MW), F32),
-            pltpu.VMEM((NY - 1, 1, MW), F32),
+            pltpu.VMEM((NY, MW), F32),
+            pltpu.VMEM((NY, MW), F32),
             dma((6,)),
             pltpu.SemaphoreType.REGULAR,
             pltpu.SemaphoreType.REGULAR,

time: 39.3 us -> 39.3 us (level)
  no operation moved by 1% of the time
where the time goes in v5:
time: 39.3 us; the launch traced here: 39.2 us
  Pallas kernels  38.7 us (98%)
  local copies, waits for them, and re-layouts  0.51 us (1%)
    pallas_call x1, Pallas kernels, local(): pl.pallas_call(kernel, out_shape=jax.ShapeDtypeStruct((1, MW), F32), in_s...  38.7 us

profile of v5, /device:TPU:1, one launch (start us, length us, event | category | flops | bytes accessed | tf_op | source)
XLA Modules:
  0.0 39.2 jit_solution(7041463121962395991)
XLA Ops:
  0.0 38.7 %shard_map.64 = f32[1,128]{1,0:T(1,128)S(1)} custom-call(bf16[64,3840]{1,0:T(8,128)(2,1)} %bitcast.6, s32[32]{0:T(128)} %flag_hbm.1, bf16[2048,256]{1,0:T(8,128)(2,1)} %bitcast.5, bf16[32,256]{1,0:T(8,128)(2,1)} %bitcast.7, bf16[32,256]{1,0:T(8,128)(2,1)} %bitcast.8, s32[2,16]{1,0:T(2,128)} %bitcast.9), custom_call_target="tpu_custom_call" | custom-call | tf_op jit(solution)/shard_map/pallas_call | solution.py:365
  38.7 0.5 %copy.8 = f32[1,128]{1,0:T(1,128)} copy(f32[1,128]{1,0:T(1,128)S(1)} %shard_map.64) | data formatting | bytes 1024
